TPU v7x, 32 devices: a whole 2x2x4 slice. The times are simulated.
32 devices in a mesh: bx: 4 (over z), by: 8 (over y, x, core).
Axes of the slice: x: 2, y: 2, z: 4, core: 2. Of those that a mesh axis runs over, the one named last changes fastest.
Arguments:
- fixed_image: bfloat16 [256, 512, 128], P('bx', 'by'), may hold values from -6 to 6
- moving_image: bfloat16 [256, 512, 128], P('bx', 'by'), may hold values from -6 to 6
- source_list: int32 [4, 8, 8], P('bx'), may hold values from 0 to 7, each once within a row
- stretch_offsets: int32 [4, 8, 2], P('bx', 'by'), may hold values from -4 to 4
Outputs:
- displacement: float32 [3, 256, 512, 128], P(None, 'bx', 'by')
- back_force: float32 [3, 256, 512, 128], P(None, 'bx', 'by')
Inputs may be any that keep to these rules, and one draw needn't show every extreme that they name: `source_list`: for each brick, its entries name every column of bricks exactly once.
All inputs are finite; a program needn't handle non-finite values.
Results may differ from a plain program's by a relative error of at most 0.004.
Values may be sent and summed in bfloat16 or wider, within the bound.
A program may use at most 320 MiB of HBM per device.

v0:
```python
import functools

import jax
import jax.numpy as jnp
import ml_dtypes
import numpy as np
from jax import lax
from jax.experimental import pallas as pl
from jax.experimental.pallas import tpu as pltpu
from jax.sharding import PartitionSpec as P

RADIUS = 8
ITERS = 3


STEP_SIZE = 128.0


def padded_2(x, sides, width):
    for axis, dim in sides:
        peers, length = (lax.axis_size(axis), x.shape[dim])
        up = [(i, (i + 1) % peers) for i in range(peers - 1)]
        down = [(j, i) for i, j in up]
        last = lax.slice_in_dim(x, length - width, length, axis=dim)
        initial = lax.slice_in_dim(x, 0, width, axis=dim)
        before = lax.ppermute(last, axis, up)
        after = lax.ppermute(initial, axis, down)
        x = jnp.concatenate([before, x, after], axis=dim)
    return x


def stretch_matrix(length, offset):
    index = jnp.arange(length).astype(jnp.float32)
    place = index + offset.astype(jnp.float32) * (2.0 * index + 1.0 - length) / (2.0 * length)
    place = jnp.clip(place, 0.0, length - 1.0)
    return jnp.maximum(0.0, 1.0 - jnp.abs(place[:, None] - index[None, :]))


def tap_weights():
    spread = 0.75 * RADIUS
    offs = np.arange(-RADIUS, RADIUS + 1).astype(np.float64)
    raw = np.exp(-offs * offs / (2.0 * spread * spread))
    raw = raw / raw.sum()
    best = None
    for scale in np.linspace(4.0, 8.0, 2001):
        near = (raw * scale).astype(ml_dtypes.bfloat16).astype(np.float64)
        err = np.sum((near / near.sum() - raw) ** 2)
        if best is None or err < best[0]:
            best = (err, near)
    near = best[1]
    return raw, near, 1.0 / near.sum()


EXACT, TAPS, UNSCALE = tap_weights()
UNSCALE = float(UNSCALE)


def band(rows, cols):
    start = (cols - rows) // 2
    dist = np.arange(cols)[None, :] - np.arange(rows)[:, None] - start
    inside = np.abs(dist) <= RADIUS
    return jnp.asarray(np.where(inside, TAPS[np.clip(dist + RADIUS, 0, 2 * RADIUS)], 0.0).astype(ml_dtypes.bfloat16))


def dot(spec, a, b):
    return jnp.einsum(spec, a, b, preferred_element_type=jnp.float32)


def halves(x):
    high = lax.reduce_precision(x, 8, 7)
    return high.astype(jnp.bfloat16), (x - high).astype(jnp.bfloat16)


def dot_split(spec, x, w):
    high, low = halves(x)
    return dot(spec, high, w) + dot(spec, low, w)


def demons_kernel(nx, ny, d0_ref, gm_ref, gn_ref, wy_ref, wz_ref, u_ref, zs, xs, xsend, xrecv, ysend, yrecv, xss, xrs, yss, yrs):
    comps, width_x, width_y, depth = gm_ref.shape
    ix, iy = lax.axis_index("bx"), lax.axis_index("by")
    has = {"bx": (ix > 0, ix < nx - 1), "by": (iy > 0, iy < ny - 1)}
    dev = {
        "bx": (lax.rem(ix + nx - 1, nx), lax.rem(ix + 1, nx)),
        "by": (lax.rem(iy + ny - 1, ny), lax.rem(iy + 1, ny)),
    }
    barrier = pltpu.get_barrier_semaphore()
    for axis in ("bx", "by"):
        for side in (0, 1):

            @pl.when(has[axis][side])
            def _():
                pl.semaphore_signal(barrier, inc=1, device_id={axis: dev[axis][side]}, device_id_type=pl.DeviceIdType.MESH)

    met = sum(ok.astype(jnp.int32) for axis in ("bx", "by") for ok in has[axis])
    pl.semaphore_wait(barrier, met)

    def copy(axis, it, side, c):
        send, recv, ss, rs = (xsend, xrecv, xss, xrs) if axis == "bx" else (ysend, yrecv, yss, yrs)
        return pltpu.make_async_remote_copy(
            src_ref=send.at[it, side, c],
            dst_ref=recv.at[it, 1 - side, c],
            send_sem=ss.at[it, side, c],
            recv_sem=rs.at[it, 1 - side, c],
            device_id={axis: dev[axis][side]},
            device_id_type=pl.DeviceIdType.MESH,
        )

    def start(axis, it, side, c):
        @pl.when(has[axis][side])
        def _():
            copy(axis, it, side, c).start()

    R = RADIUS
    for side in (0, 1):
        at_x = 0 if side == 0 else R + width_x
        at_y = 0 if side == 0 else R + width_y

        @pl.when(jnp.logical_not(has["bx"][side]))
        def _():
            for c in range(comps):
                zs[c, at_x : at_x + R] = jnp.zeros((R, width_y, depth), jnp.float32)

        @pl.when(jnp.logical_not(has["by"][side]))
        def _():
            for c in range(comps):
                xs[c, :, at_y : at_y + R, :] = jnp.zeros((width_x, R, depth), jnp.float32)

    def field_pair(x):
        rhs = jnp.concatenate([xs[c, x + r] for c in range(comps) for r in range(2)], axis=1).astype(jnp.bfloat16)
        out = jnp.dot(wy_ref[...], rhs, preferred_element_type=jnp.float32) * UNSCALE
        return [[out[:, (2 * c + r) * depth : (2 * c + r + 1) * depth] for c in range(comps)] for r in range(2)]

    def force_pair(x, it):
        field = field_pair(x) if it else None
        parts = [None] * (2 * comps)
        for r in range(2):
            differ = d0_ref[x + r]
            grads = [gn_ref[c, x + r] for c in range(comps)]
            denom = 1.0
            for c in range(comps):
                denom = denom + grads[c] * grads[c]
                if it:
                    differ = differ + field[r][c] * gm_ref[c, x + r]
            gain = STEP_SIZE * (differ / (denom + differ * differ))
            for c in range(comps):
                pushed_c = gain * grads[c]
                if it:
                    pushed_c = pushed_c + field[r][c]
                high = pushed_c.astype(jnp.bfloat16)
                low = (pushed_c - high.astype(jnp.float32)).astype(jnp.bfloat16)
                parts[2 * c + r] = jnp.concatenate([high, low], axis=1)
        lhs = jnp.concatenate(parts, axis=0)
        out = jnp.dot(lhs, wz_ref[...], preferred_element_type=jnp.float32) * UNSCALE
        for c in range(comps):
            for r in range(2):
                at = (2 * c + r) * width_y
                zs[c, R + x + r] = out[at : at + width_y]

    half = R // 2
    pairs = width_x // 2
    blocks_x, blocks_y = width_x // R, width_y // R
    for it in range(ITERS):

        @pl.loop(0, 2 * half)
        def _(p):
            force_pair(2 * (p + (p // half) * (pairs - 2 * half)), it)

        for c in range(comps):
            for side in (0, 1):
                at = R if side == 0 else width_x
                xsend[it, side, c] = zs[c, at : at + R].astype(jnp.bfloat16)
                start("bx", it, side, c)

        @pl.loop(half, pairs - half)
        def _(p):
            force_pair(2 * p, it)

        for c in range(comps):
            for side in (0, 1):
                at = 0 if side == 0 else R + width_x

                @pl.when(has["bx"][side])
                def _():
                    copy("bx", it, 1 - side, c).wait_recv()
                    zs[c, at : at + R] = xrecv[it, side, c].astype(jnp.float32)

            @pl.loop(0, blocks_x * blocks_y)
            def _(t):
                x0 = (t // blocks_y) * R
                y0 = pl.multiple_of((t % blocks_y) * R, R)
                block = zs[c, pl.ds(x0, 3 * R), pl.ds(y0, R), :]
                total = block[R : 2 * R] * float(EXACT[R])
                for d in range(1, R + 1):
                    total = total + (block[R - d : 2 * R - d] + block[R + d : 2 * R + d]) * float(EXACT[R + d])
                xs[c, pl.ds(x0, R), pl.ds(pl.multiple_of(y0 + R, R), R), :] = total

            @pl.loop(0, blocks_x)
            def _(t):
                for side in (0, 1):
                    at = R if side == 0 else width_y
                    edge = xs[c, pl.ds(t * R, R), at : at + R, :]
                    ysend[it, side, c, pl.ds(t * half, half)] = edge.reshape(half, 2 * R, depth).astype(jnp.bfloat16)

            for side in (0, 1):
                start("by", it, side, c)

        for c in range(comps):
            for side in (0, 1):
                at = 0 if side == 0 else R + width_y

                @pl.when(has["by"][side])
                def _():
                    copy("by", it, 1 - side, c).wait_recv()

                    @pl.loop(0, blocks_x)
                    def _(t):
                        got = yrecv[it, side, c, pl.ds(t * half, half)].astype(jnp.float32)
                        xs[c, pl.ds(t * R, R), at : at + R, :] = got.reshape(R, R, depth)

    @pl.loop(0, pairs)
    def _(p):
        field = field_pair(2 * p)
        for r in range(2):
            for c in range(comps):
                u_ref[c, 2 * p + r] = field[r][c]

    for it in range(ITERS):
        for axis in ("bx", "by"):
            for side in (0, 1):
                for c in range(comps):

                    @pl.when(has[axis][side])
                    def _():
                        copy(axis, it, side, c).wait_send()


def demons(d0, gm, gn):
    comps, width_x, width_y, depth = gm.shape
    grid_x, grid_y = lax.axis_size("bx"), lax.axis_size("by")
    wz = band(depth, depth)
    vmem = pl.BlockSpec(memory_space=pltpu.VMEM)
    edge_x = pltpu.VMEM((ITERS, 2, comps, RADIUS, width_y, depth), jnp.bfloat16)
    edge_y = pltpu.VMEM((ITERS, 2, comps, width_x // 2, 2 * RADIUS, depth), jnp.bfloat16)
    sems = pltpu.SemaphoreType.DMA((ITERS, 2, comps))
    return pl.pallas_call(
        functools.partial(demons_kernel, grid_x, grid_y),
        out_shape=jax.ShapeDtypeStruct(gm.shape, jnp.float32),
        in_specs=[vmem] * 5,
        out_specs=vmem,
        scratch_shapes=[
            pltpu.VMEM((comps, width_x + 2 * RADIUS, width_y, depth), jnp.float32),
            pltpu.VMEM((comps, width_x, width_y + 2 * RADIUS, depth), jnp.float32),
            edge_x,
            edge_x,
            edge_y,
            edge_y,
            sems,
            sems,
            sems,
            sems,
        ],
        compiler_params=pltpu.CompilerParams(collective_id=0, has_side_effects=True, vmem_limit_bytes=60 << 20),
    )(d0, gm, gn, band(width_y, width_y + 2 * RADIUS), jnp.concatenate([wz, wz], axis=0))


def central(padded):
    zpad = jnp.pad(padded, ((0, 0), (0, 0), (1, 1)))
    grad_x = (zpad[2:, 1:-1, 1:-1] - zpad[:-2, 1:-1, 1:-1]) * 0.5
    grad_y = (zpad[1:-1, 2:, 1:-1] - zpad[1:-1, :-2, 1:-1]) * 0.5
    grad_z = (zpad[1:-1, 1:-1, 2:] - zpad[1:-1, 1:-1, :-2]) * 0.5
    return jnp.stack([grad_x, grad_y, grad_z])


def local(fixed_image, moving_image, source_list, stretch_offsets):
    width_x, width_y, depth = fixed_image.shape
    peers = lax.axis_size("by")
    mine = lax.axis_index("by")
    rows_slab = width_x // peers
    lists = source_list[0]
    own_list = lax.dynamic_index_in_dim(lists, mine, 0, keepdims=False)
    slab_ids = jnp.arange(peers)
    asked = (lists == mine).astype(jnp.int32)
    wanted = jnp.sum(asked * slab_ids[None, :], axis=1)
    slabs = moving_image.reshape(peers, rows_slab, width_y, depth)
    outgoing = jnp.take(slabs, wanted, axis=0)
    incoming = lax.all_to_all(outgoing, "by", split_axis=0, concat_axis=0, tiled=True)
    offsets = stretch_offsets[0, 0]
    stretch_y = stretch_matrix(width_y, offsets[0])
    stretch_z = stretch_matrix(depth, offsets[1])
    first = jnp.einsum(
        "yc,pxcz->pxyz",
        stretch_y.astype(jnp.bfloat16),
        incoming,
        preferred_element_type=jnp.float32,
    )
    second = dot_split("pxyz,wz->pxyw", first, stretch_z.astype(jnp.bfloat16))
    stretched = second.astype(jnp.bfloat16)
    warped = jnp.take(stretched, own_list, axis=0).reshape(width_x, width_y, depth)
    stacked = jnp.stack([fixed_image, warped])
    grown = padded_2(stacked, (("bx", 1), ("by", 2)), 1)
    grad_moving = central(grown[1].astype(jnp.float32))
    grad_mean = 0.5 * (central(grown[0].astype(jnp.float32)) + grad_moving)
    fixed_f = fixed_image.astype(jnp.float32)
    warped_f = warped.astype(jnp.float32)
    field_u = demons(warped_f - fixed_f, grad_moving, grad_mean)
    pieces_u = field_u.reshape(3, peers, rows_slab, width_y, depth)
    turned = dot_split("ckxyz,yv->ckxvz", pieces_u, stretch_y.astype(jnp.bfloat16))
    turned = dot_split("ckxvz,zw->ckxvw", turned, stretch_z.astype(jnp.bfloat16)).astype(jnp.bfloat16)
    inverse = jnp.sum(
        (own_list[None, :] == slab_ids[:, None]).astype(jnp.int32) * slab_ids[None, :], axis=1
    )
    sending = jnp.take(turned, inverse, axis=1)
    arriving = lax.all_to_all(sending, "by", split_axis=1, concat_axis=1, tiled=True)
    table = asked.astype(jnp.bfloat16)
    back = jnp.einsum("tk,ctxyz->ckxyz", table, arriving, preferred_element_type=jnp.float32)
    back_force = back.reshape(3, width_x, width_y, depth)
    return (field_u, back_force)


def solution(mesh):
    return jax.shard_map(
        local,
        mesh=mesh,
        in_specs=(
            P("bx", "by", None),
            P("bx", "by", None),
            P("bx", None, None),
            P("bx", "by", None),
        ),
        out_specs=(P(None, "bx", "by", None), P(None, "bx", "by", None)),
        check_vma=False,
    )
```

profile of v0, /device:TPU:1, one launch (start us, length us, event | category | flops | bytes accessed | tf_op | source)
XLA Modules:
  0.0 208.2 jit_solution(3090196661389507969)
XLA Ops:
  2.6 1.1 broadcast_select_fusion.1
  3.8 5.2 %all-to-all-start = ((bf16[8,8,64,128]{3,2,1,0:T(8,128)(2,1)}), bf16[8,8,64,128]{3,2,1,0:T(8,128)(2,1)S(1)}, u32[]{:S(2)}, u32[]{:S(2)}) async-start(bf16[8,8,64,128]{3,2,1,0:T(8,128)(2,1)} %broadcast_select_fusion.1), calls=%async_computation | async-start | bytes 2097152 | tf_op jit(solution)/shard_map/all_to_all | solution.py:287
  11.7 9.3 %all-to-all-done = bf16[8,8,64,128]{3,2,1,0:T(8,128)(2,1)S(1)} async-done(((bf16[8,8,64,128]{3,2,1,0:T(8,128)(2,1)}), bf16[8,8,64,128]{3,2,1,0:T(8,128)(2,1)S(1)}, u32[]{:S(2)}, u32[]{:S(2)}) %all-to-all-start) | async-done | bytes 1048608 | tf_op jit(solution)/shard_map/all_to_all | solution.py:287
  23.8 3.2 %collective-permute-start = (bf16[2,1,64,128]{3,2,1,0:T(8,128)(2,1)S(1)}, bf16[2,1,64,128]{3,2,1,0:T(8,128)(2,1)S(1)}, u32[]{:S(2)}, u32[]{:S(2)}) collective-permute-start(bf16[2,1,64,128]{3,2,1,0:T(8,128)(2,1)S(1)} %get-tuple-element.19), channel_id=1, source_target_pairs={{0,8},{8,16},{16,24},{1,9},{9,17},{17,25},{2,10},{10,18},{18,26},{... | collective-permute-start | bytes 98312 | tf_op jit(solution)/shard_map/ppermute | solution.py:26
  27.0 1.3 collective-permute-start.1
  28.3 3.3 %collective-permute-done.1 = bf16[2,1,64,128]{3,2,1,0:T(8,128)(2,1)S(1)} collective-permute-done((bf16[2,1,64,128]{3,2,1,0:T(8,128)(2,1)S(1)}, bf16[2,1,64,128]{3,2,1,0:T(8,128)(2,1)S(1)}, u32[]{:S(2)}, u32[]{:S(2)}) %collective-permute-start.1) | collective-permute-done | bytes 32800 | tf_op jit(solution)/shard_map/ppermute | solution.py:27
  31.8 6.9 %collective-permute-start.2 = (bf16[2,66,1,128]{3,2,1,0:T(2,128)(2,1)S(1)}, bf16[2,66,1,128]{3,2,1,0:T(2,128)(2,1)S(1)}, u32[]{:S(2)}, u32[]{:S(2)}) collective-permute-start(bf16[2,66,1,128]{3,2,1,0:T(2,128)(2,1)S(1)} %get-tuple-element.17), channel_id=1, source_target_pairs={{0,1},{1,2},{2,3},{3,4},{4,5},{5,6},{6,7},{8,9},{9,10},{10,11},{11... | collective-permute-start | bytes 101384 | tf_op jit(solution)/shard_map/ppermute | solution.py:26
  38.7 1.9 collective-permute-start.3
  40.6 1.8 convert_subtract_fusion.d0_ref
  42.4 1.9 collective-permute-done.3
  44.3 2.5 %pad_maximum_fusion.1 = bf16[2,66,66,128]{3,2,1,0:T(8,128)(2,1)S(1)} fusion(bf16[2,66,1,128]{3,2,1,0:T(2,128)(2,1)S(1)} %collective-permute-done.3, bf16[2,1,64,128]{3,2,1,0:T(8,128)(2,1)S(1)} %collective-permute-done.1, bf16[1,64,64,128]{3,2,1,0:T(8,128)(2,1)S(1)} %bitcast.93, bf16[1,64,64,128]{3,2,1,0:T(8,128)(2,1)S(1)} %bitcast.96, ...), kind=kLoop, calls=%fused_computation.29 | loop fusion | flops 13381632 | bytes 4460544 | tf_op jit(solution)/shard_map/concatenate | solution.py:28
  47.1 5.6 %fusion.26 = (f32[1,64,64,128]{3,2,1,0:T(8,128)S(1)}, f32[1,64,64,128]{3,2,1,0:T(8,128)S(1)}, f32[1,64,64,128]{3,2,1,0:T(8,128)S(1)}, f32[1,64,64,128]{3,2,1,0:T...) fusion(f32[66,66,128]{2,1,0:T(8,128)S(1)} %get-tuple-element.12, ...), kind=kLoop, calls=%fused_computation.42 | loop fusion | flops 6291456 | bytes 34226176 | tf_op jit(solution)/shard_map/stack | solution.py:272
  52.8 6.8 %fusion.2 = (f32[3,64,64,128]{3,2,1,0:T(8,128)}, f32[3,64,64,128]{3,2,1,0:T(8,128)}) fusion(f32[1,64,64,128]{3,2,1,0:T(8,128)S(1)} %get-tuple-element.10, f32[1,64,64,128]{3,2,1,0:T(8,128)S(1)} %get-tuple-element.11, f32[1,64,64,128]{3,2,1,0:T(8,128)S(1)} %get-tuple-element.9, f32[1,64,64,128]{3,2,1,0:T(8,128)S(1)} %get-tuple-element.24, ...), kind=kLoop, calls=%fused_computation.11 | loop fusion | flops 9437184 | bytes 25165824 | tf_op jit(solution)/shard_map/mul | solution.py:303
  59.6 86.3 %shard_map.77 = f32[3,64,64,128]{3,2,1,0:T(8,128)} custom-call(f32[64,64,128]{2,1,0:T(8,128)} %convert_subtract_fusion.d0_ref, f32[3,64,64,128]{3,2,1,0:T(8,128)} %get-tuple-element.8.gm_ref, f32[3,64,64,128]{3,2,1,0:T(8,128)} %get-tuple-element.7.gn_ref, bf16[64,80]{1,0:T(8,128)(2,1)} %constant.77.clone.wy_ref, bf16[256,128]{1,0:T(8,128)(2,1)} %constant.84.wz_ref), custom_call_target="tpu_custom_call" | custom-call | tf_op jit(solution)/shard_map/pallas_call | solution.py:246
  145.9 4.0 %fusion.5 = f32[64,3,8,8,128]{4,0,3,2,1:T(8,128)S(1)} fusion(f32[3,8,8,64,128]{4,3,2,1,0:T(8,128)} %bitcast.87, f32[64]{0:T(128)S(1)} %iota_convert_fusion.1, f32[64]{0:T(128)S(1)} %add_clamp_fusion.1), kind=kOutput, calls=%fused_computation.18 | convolution fusion | flops 206065664 | bytes 12583424 | tf_op jit(solution)/shard_map/ckxyz,yv->ckxvz/dot_general | solution.py:66
  150.4 1.0 fusion.7
  151.5 1.1 fusion.3
  152.5 1.1 add_convert_fusion
  153.6 2.6 %gather_fusion = bf16[8,3,8,64,128]{4,3,2,1,0:T(8,128)(2,1)} fusion(bf16[3,8,8,64,128]{4,3,2,1,0:T(8,128)(2,1)S(1)} %add_convert_fusion, s32[1024]{0:T(1024)S(1)} %pad_clamp_fusion), kind=kCustom, calls=%fused_computation.2 | custom fusion | bytes 6291488 | tf_op jit(solution)/shard_map/jit(_take)/gather | solution.py:313
  156.2 2.3 %select_bitcast_fusion = bf16[3,8,8,64,128]{4,3,2,0,1:T(8,128)(2,1)S(1)} fusion(bf16[8,3,8,64,128]{4,3,2,1,0:T(8,128)(2,1)} %gather_fusion, pred[8]{0:T(512)(128)(4,1)S(1)} %compare_and_fusion.2), kind=kLoop, calls=%fused_computation.23 | loop fusion | flops 1572864 | bytes 6291464 | tf_op jit(solution)/shard_map/jit(_take)/select_n | solution.py:313
  158.5 41.2 %all_to_all.10 = bf16[3,8,8,64,128]{4,3,2,0,1:T(8,128)(2,1)S(1)} all-to-all(bf16[3,8,8,64,128]{4,3,2,0,1:T(8,128)(2,1)S(1)} %select_bitcast_fusion), channel_id=1, replica_groups=mesh['bx'=4,'by'=8] {'by'}, dimensions={1} | all-to-all | bytes 6291456 | tf_op jit(solution)/shard_map/all_to_all | solution.py:314
  199.7 1.9 fusion.13
  201.7 3.8 %copy.17 = f32[3,8,8,64,128]{4,3,2,1,0:T(8,128)} copy(f32[3,8,8,64,128]{4,1,3,2,0:T(8,128)S(1)} %fusion.13) | data formatting | bytes 12582912 | tf_op jit(solution)/shard_map/tk,ctxyz->ckxyz/transpose | solution.py:316
  205.5 2.7 %copy.30 = f32[3,64,64,128]{3,2,1,0:T(8,128)} copy(f32[3,64,64,128]{3,2,1,0:T(8,128)S(1)} %bitcast.90) | data formatting | bytes 12582912
  (42 shorter events, 7.3 us)
Async XLA Ops:
  0.6 1.2 copy-start
  1.9 7.1 %copy-start.4 = (s32[1,1,2]{2,1,0:T(1,128)S(1)}, s32[1,1,2]{2,1,0:T(1,128)}, u32[]{:S(2)}) copy-start(s32[1,1,2]{2,1,0:T(1,128)} %param.11) | copy-start | bytes 28
  3.8 17.2 %all-to-all-start = ((bf16[8,8,64,128]{3,2,1,0:T(8,128)(2,1)}), bf16[8,8,64,128]{3,2,1,0:T(8,128)(2,1)S(1)}, u32[]{:S(2)}, u32[]{:S(2)}) async-start(bf16[8,8,64,128]{3,2,1,0:T(8,128)(2,1)} %broadcast_select_fusion.1), calls=%async_computation | async-start | bytes 2097152 | tf_op jit(solution)/shard_map/all_to_all | solution.py:287
  22.6 1.2 copy-start.3
  23.8 4.5 %collective-permute-start = (bf16[2,1,64,128]{3,2,1,0:T(8,128)(2,1)S(1)}, bf16[2,1,64,128]{3,2,1,0:T(8,128)(2,1)S(1)}, u32[]{:S(2)}, u32[]{:S(2)}) collective-permute-start(bf16[2,1,64,128]{3,2,1,0:T(8,128)(2,1)S(1)} %get-tuple-element.19), channel_id=1, source_target_pairs={{0,8},{8,16},{16,24},{1,9},{9,17},{17,25},{2,10},{10,18},{18,26},{... | collective-permute-start | bytes 98312 | tf_op jit(solution)/shard_map/ppermute | solution.py:26
  27.0 4.7 %collective-permute-start.1 = (bf16[2,1,64,128]{3,2,1,0:T(8,128)(2,1)S(1)}, bf16[2,1,64,128]{3,2,1,0:T(8,128)(2,1)S(1)}, u32[]{:S(2)}, u32[]{:S(2)}) collective-permute-start(bf16[2,1,64,128]{3,2,1,0:T(8,128)(2,1)S(1)} %get-tuple-element.20), channel_id=1, source_target_pairs={{8,0},{16,8},{24,16},{9,1},{17,9},{25,17},{10,2},{18,10},{26,18},{... | collective-permute-start | bytes 98312 | tf_op jit(solution)/shard_map/ppermute | solution.py:27
  31.8 10.7 %collective-permute-start.2 = (bf16[2,66,1,128]{3,2,1,0:T(2,128)(2,1)S(1)}, bf16[2,66,1,128]{3,2,1,0:T(2,128)(2,1)S(1)}, u32[]{:S(2)}, u32[]{:S(2)}) collective-permute-start(bf16[2,66,1,128]{3,2,1,0:T(2,128)(2,1)S(1)} %get-tuple-element.17), channel_id=1, source_target_pairs={{0,1},{1,2},{2,3},{3,4},{4,5},{5,6},{6,7},{8,9},{9,10},{10,11},{11... | collective-permute-start | bytes 101384 | tf_op jit(solution)/shard_map/ppermute | solution.py:26
  38.7 5.6 %collective-permute-start.3 = (bf16[2,66,1,128]{3,2,1,0:T(2,128)(2,1)S(1)}, bf16[2,66,1,128]{3,2,1,0:T(2,128)(2,1)S(1)}, u32[]{:S(2)}, u32[]{:S(2)}) collective-permute-start(bf16[2,66,1,128]{3,2,1,0:T(2,128)(2,1)S(1)} %get-tuple-element.18), channel_id=1, source_target_pairs={{1,0},{2,1},{3,2},{4,3},{5,4},{6,5},{7,6},{9,8},{10,9},{11,10},{12... | collective-permute-start | bytes 101384 | tf_op jit(solution)/shard_map/ppermute | solution.py:27
  145.8 4.6 %copy-start.2 = (f32[3,64,64,128]{3,2,1,0:T(8,128)S(1)}, f32[3,64,64,128]{3,2,1,0:T(8,128)}, u32[]{:S(2)}) copy-start(f32[3,64,64,128]{3,2,1,0:T(8,128)} %shard_map.77) | copy-start | bytes 18874372
  199.7 5.7 %slice-start = ((s8[6291456]{0:T(1024)(128)(4,1)}), s8[4194304]{0:T(1024)(128)(4,1)S(1)}, s32[]{:S(2)}) async-start(s8[6291456]{0:T(1024)(128)(4,1)} %bitcast.89), calls=%async_computation.2 | async-start | bytes 8388608
  201.7 3.8 %slice-start.1 = ((s8[6291456]{0:T(1024)(128)(4,1)}), s8[2097152]{0:T(1024)(128)(4,1)S(1)}, s32[]{:S(2)}) async-start(s8[6291456]{0:T(1024)(128)(4,1)} %bitcast.89), calls=%async_computation.3 | async-start | bytes 4194304
  205.5 2.7 %copy-start.1 = (bf16[64,64,128]{2,1,0:T(8,128)(2,1)S(1)}, bf16[64,64,128]{2,1,0:T(8,128)(2,1)}, u32[]{:S(2)}) copy-start(bf16[64,64,128]{2,1,0:T(8,128)(2,1)} %param.9) | copy-start | bytes 3145732
where the time goes:
time: 210 us; the launch traced here: 208 us
  Pallas kernels  86.3 us (41%)
  blocking collectives  41.2 us (20%)
  other arithmetic  22.5 us (11%)
  starting transfers between devices  18.6 us (9%)
  waiting for transfers between devices  14.5 us (7%)
  local copies, waits for them, and re-layouts  12.4 us (6%)
  matrix products  10.7 us (5%)
    pallas_call x1, Pallas kernels, demons(): pl.pallas_call(functools.partial(demons_kernel, grid_x, grid_y), out_shap...  86.3 us
    all_to_all x1, blocking collectives, local(): lax.all_to_all(sending, 'by', split_axis=1, concat_axis=1, tiled=True)  41.2 us
    ppermute x2, starting transfers between devices, padded_2(): before = lax.ppermute(last, axis, up)  10.1 us
    all_to_all x1, waiting for transfers between devices, local(): lax.all_to_all(outgoing, 'by', split_axis=0, concat_axis=0, tiled=True)  9.27 us
    dot_general x6, matrix products, dot(): return jnp.einsum(spec, a, b, preferred_element_type=jnp.float32)  8.17 us
    mul x1, other arithmetic, local(): grad_mean = 0.5 * (central(grown[0].astype(jnp.float32)) + grad_moving)  6.8 us
    another operation x1, other arithmetic, central(): return jnp.stack([grad_x, grad_y, grad_z])  5.64 us
    all_to_all x1, starting transfers between devices, local(): lax.all_to_all(outgoing, 'by', split_axis=0, concat_axis=0, tiled=True)  5.22 us
  transfers between devices with their start and end apart: 5, of which 3 were waited for; matrix products, arithmetic and copies ran while one was open for 2% of the time, Pallas kernels for 0%

commit v1 on v0

--- a/solution.py
+++ b/solution.py
@@ -14,19 +14,6 @@
 
 
 STEP_SIZE = 128.0
-
-
-def padded_2(x, sides, width):
-    for axis, dim in sides:
-        peers, length = (lax.axis_size(axis), x.shape[dim])
-        up = [(i, (i + 1) % peers) for i in range(peers - 1)]
-        down = [(j, i) for i, j in up]
-        last = lax.slice_in_dim(x, length - width, length, axis=dim)
-        initial = lax.slice_in_dim(x, 0, width, axis=dim)
-        before = lax.ppermute(last, axis, up)
-        after = lax.ppermute(initial, axis, down)
-        x = jnp.concatenate([before, x, after], axis=dim)
-    return x
 
 
 def stretch_matrix(length, offset):
@@ -76,7 +63,7 @@
     return dot(spec, high, w) + dot(spec, low, w)
 
 
-def demons_kernel(nx, ny, d0_ref, gm_ref, gn_ref, wy_ref, wz_ref, u_ref, zs, xs, xsend, xrecv, ysend, yrecv, xss, xrs, yss, yrs):
+def demons_kernel(nx, ny, order, fixed_ref, warped_ref, wy_ref, wz_ref, sy_ref, sz_ref, u_ref, back_ref, d0_ref, gm_ref, gn_ref, tsend, esx, erx, esy, ery, ess, ers, tss, trs, own_sem, zs, xs, xsend, xrecv, ysend, yrecv, xss, xrs, yss, yrs):
     comps, width_x, width_y, depth = gm_ref.shape
     ix, iy = lax.axis_index("bx"), lax.axis_index("by")
     has = {"bx": (ix > 0, ix < nx - 1), "by": (iy > 0, iy < ny - 1)}
@@ -85,15 +72,91 @@
         "by": (lax.rem(iy + ny - 1, ny), lax.rem(iy + 1, ny)),
     }
     barrier = pltpu.get_barrier_semaphore()
-    for axis in ("bx", "by"):
+    for side in (0, 1):
+
+        @pl.when(has["bx"][side])
+        def _():
+            pl.semaphore_signal(barrier, inc=1, device_id={"bx": dev["bx"][side]}, device_id_type=pl.DeviceIdType.MESH)
+
+    for j in range(1, ny):
+        pl.semaphore_signal(barrier, inc=1, device_id={"by": lax.rem(iy + j, ny)}, device_id_type=pl.DeviceIdType.MESH)
+    met = sum(ok.astype(jnp.int32) for ok in has["bx"]) + (ny - 1)
+    pl.semaphore_wait(barrier, met)
+
+    R = RADIUS
+
+    def edge_copy(n, axis, side):
+        send, recv = (esx, erx) if axis == "bx" else (esy, ery)
+        return pltpu.make_async_remote_copy(
+            src_ref=send.at[side],
+            dst_ref=recv.at[1 - side],
+            send_sem=ess.at[n, side],
+            recv_sem=ers.at[n, 1 - side],
+            device_id={axis: dev[axis][side]},
+            device_id_type=pl.DeviceIdType.MESH,
+        )
+
+    images = (fixed_ref, warped_ref)
+    for m in range(2):
+        esx[0, m] = images[m][0]
+        esx[1, m] = images[m][width_x - 1]
+
+    @pl.loop(0, width_x)
+    def _(x):
+        for m in range(2):
+            row = images[m][x].astype(jnp.float32)
+            zs[m, R + x] = row
+            esy[0, m, pl.ds(x, 1), :] = row[0:1]
+            esy[1, m, pl.ds(x, 1), :] = row[width_y - 1 : width_y]
+
+    for n, axis in enumerate(("bx", "by")):
         for side in (0, 1):
 
             @pl.when(has[axis][side])
             def _():
-                pl.semaphore_signal(barrier, inc=1, device_id={axis: dev[axis][side]}, device_id_type=pl.DeviceIdType.MESH)
-
-    met = sum(ok.astype(jnp.int32) for axis in ("bx", "by") for ok in has[axis])
-    pl.semaphore_wait(barrier, met)
+                edge_copy(n, axis, side).start()
+
+    for side in (0, 1):
+        at = R - 1 if side == 0 else R + width_x
+
+        @pl.when(has["bx"][side])
+        def _():
+            edge_copy(0, "bx", 1 - side).wait_recv()
+            for m in range(2):
+                zs[m, at] = erx[side, m].astype(jnp.float32)
+
+        @pl.when(jnp.logical_not(has["bx"][side]))
+        def _():
+            for m in range(2):
+                zs[m, at] = jnp.zeros((width_y, depth), jnp.float32)
+
+        @pl.when(has["by"][side])
+        def _():
+            edge_copy(1, "by", 1 - side).wait_recv()
+
+        @pl.when(jnp.logical_not(has["by"][side]))
+        def _():
+            ery[side] = jnp.zeros(ery.shape[1:], jnp.float32)
+
+    at_y = lax.broadcasted_iota(jnp.int32, (width_y, depth), 0)
+    at_z = lax.broadcasted_iota(jnp.int32, (width_y, depth), 1)
+
+    @pl.loop(0, width_x)
+    def _(x):
+        both = []
+        for m in range(2):
+            row = zs[m, R + x]
+            grad_x = (zs[m, R + x + 1] - zs[m, R + x - 1]) * 0.5
+            low = jnp.where(at_y == 0, ery[0, m, pl.ds(x, 1), :], pltpu.roll(row, 1, 0))
+            high = jnp.where(at_y == width_y - 1, ery[1, m, pl.ds(x, 1), :], pltpu.roll(row, width_y - 1, 0))
+            grad_y = (high - low) * 0.5
+            low = jnp.where(at_z == 0, 0.0, pltpu.roll(row, 1, 1))
+            high = jnp.where(at_z == depth - 1, 0.0, pltpu.roll(row, depth - 1, 1))
+            both.append((grad_x, grad_y, (high - low) * 0.5))
+        for c in range(comps):
+            gm_ref[c, x] = both[1][c]
+            gn_ref[c, x] = 0.5 * (both[0][c] + both[1][c])
+        d0_ref[x] = zs[1, R + x] - zs[0, R + x]
 
     def copy(axis, it, side, c):
         send, recv, ss, rs = (xsend, xrecv, xss, xrs) if axis == "bx" else (ysend, yrecv, yss, yrs)
@@ -111,7 +174,6 @@
         def _():
             copy(axis, it, side, c).start()
 
-    R = RADIUS
     for side in (0, 1):
         at_x = 0 if side == 0 else R + width_x
         at_y = 0 if side == 0 else R + width_y
@@ -225,6 +287,61 @@
             for c in range(comps):
                 u_ref[c, 2 * p + r] = field[r][c]
 
+    slab = width_x // ny
+
+    def halves_of(x):
+        high = x.astype(jnp.bfloat16)
+        return high, (x - high.astype(jnp.float32)).astype(jnp.bfloat16)
+
+    def turn(d):
+        first_row = order[d] * slab
+
+        @pl.loop(0, slab // 2)
+        def _(p):
+            x = first_row + 2 * p
+            rows = jnp.concatenate([u_ref[c, x + r] for c in range(comps) for r in range(2)], axis=1)
+            mid = jnp.dot(sy_ref[...], jnp.concatenate(halves_of(rows), axis=0), preferred_element_type=jnp.float32)
+            parts = []
+            for k in range(2 * comps):
+                parts.append(jnp.concatenate(halves_of(mid[:, k * depth : (k + 1) * depth]), axis=1))
+            out = jnp.dot(jnp.concatenate(parts, axis=0), sz_ref[...], preferred_element_type=jnp.float32)
+            for c in range(comps):
+                for r in range(2):
+                    at = (2 * c + r) * width_y
+                    tsend[d, c, 2 * p + r] = out[at : at + width_y].astype(jnp.bfloat16)
+
+    def slab_copy(j):
+        d = lax.rem(iy + j, ny)
+        return pltpu.make_async_remote_copy(
+            src_ref=tsend.at[d],
+            dst_ref=back_ref.at[iy],
+            send_sem=tss.at[j],
+            recv_sem=trs.at[j],
+            device_id={"by": d},
+            device_id_type=pl.DeviceIdType.MESH,
+        )
+
+    @pl.loop(1, ny)
+    def _(j):
+        turn(lax.rem(iy + j, ny))
+        slab_copy(j).start()
+
+    turn(iy)
+    own = pltpu.make_async_copy(tsend.at[iy], back_ref.at[iy], own_sem)
+    own.start()
+    own.wait()
+
+    @pl.loop(1, ny)
+    def _(j):
+        slab_copy(j).wait()
+
+    for n, axis in enumerate(("bx", "by")):
+        for side in (0, 1):
+
+            @pl.when(has[axis][side])
+            def _():
+                edge_copy(n, axis, side).wait_send()
+
     for it in range(ITERS):
         for axis in ("bx", "by"):
             for side in (0, 1):
@@ -235,20 +352,43 @@
                         copy(axis, it, side, c).wait_send()
 
 
-def demons(d0, gm, gn):
-    comps, width_x, width_y, depth = gm.shape
+def demons(order, fixed, warped, stretch_y, stretch_z):
+    comps = 3
+    width_x, width_y, depth = fixed.shape
     grid_x, grid_y = lax.axis_size("bx"), lax.axis_size("by")
     wz = band(depth, depth)
+    sy = stretch_y.T.astype(jnp.bfloat16)
+    sz = stretch_z.astype(jnp.bfloat16)
+    full = pltpu.VMEM((comps, width_x, width_y, depth), jnp.float32)
+    slabs = (grid_y, comps, width_x // grid_y, width_y, depth)
+    edge_1 = pltpu.VMEM((2, 2, width_y, depth), jnp.bfloat16)
+    edge_2 = pltpu.VMEM((2, 2, width_x, depth), jnp.float32)
     vmem = pl.BlockSpec(memory_space=pltpu.VMEM)
     edge_x = pltpu.VMEM((ITERS, 2, comps, RADIUS, width_y, depth), jnp.bfloat16)
     edge_y = pltpu.VMEM((ITERS, 2, comps, width_x // 2, 2 * RADIUS, depth), jnp.bfloat16)
     sems = pltpu.SemaphoreType.DMA((ITERS, 2, comps))
     return pl.pallas_call(
         functools.partial(demons_kernel, grid_x, grid_y),
-        out_shape=jax.ShapeDtypeStruct(gm.shape, jnp.float32),
-        in_specs=[vmem] * 5,
-        out_specs=vmem,
+        out_shape=(
+            jax.ShapeDtypeStruct((comps, width_x, width_y, depth), jnp.float32),
+            jax.ShapeDtypeStruct(slabs, jnp.bfloat16),
+        ),
+        in_specs=[pl.BlockSpec(memory_space=pltpu.SMEM)] + [vmem] * 6,
+        out_specs=(vmem, pl.BlockSpec(memory_space=pl.ANY)),
         scratch_shapes=[
+            pltpu.VMEM((width_x, width_y, depth), jnp.float32),
+            full,
+            full,
+            pltpu.VMEM(slabs, jnp.bfloat16),
+            edge_1,
+            edge_1,
+            edge_2,
+            edge_2,
+            pltpu.SemaphoreType.DMA((2, 2)),
+            pltpu.SemaphoreType.DMA((2, 2)),
+            pltpu.SemaphoreType.DMA((grid_y,)),
+            pltpu.SemaphoreType.DMA((grid_y,)),
+            pltpu.SemaphoreType.DMA,
             pltpu.VMEM((comps, width_x + 2 * RADIUS, width_y, depth), jnp.float32),
             pltpu.VMEM((comps, width_x, width_y + 2 * RADIUS, depth), jnp.float32),
             edge_x,
@@ -260,16 +400,16 @@
             sems,
             sems,
         ],
-        compiler_params=pltpu.CompilerParams(collective_id=0, has_side_effects=True, vmem_limit_bytes=60 << 20),
-    )(d0, gm, gn, band(width_y, width_y + 2 * RADIUS), jnp.concatenate([wz, wz], axis=0))
-
-
-def central(padded):
-    zpad = jnp.pad(padded, ((0, 0), (0, 0), (1, 1)))
-    grad_x = (zpad[2:, 1:-1, 1:-1] - zpad[:-2, 1:-1, 1:-1]) * 0.5
-    grad_y = (zpad[1:-1, 2:, 1:-1] - zpad[1:-1, :-2, 1:-1]) * 0.5
-    grad_z = (zpad[1:-1, 1:-1, 2:] - zpad[1:-1, 1:-1, :-2]) * 0.5
-    return jnp.stack([grad_x, grad_y, grad_z])
+        compiler_params=pltpu.CompilerParams(collective_id=0, has_side_effects=True, vmem_limit_bytes=62 << 20),
+    )(
+        order,
+        fixed,
+        warped,
+        band(width_y, width_y + 2 * RADIUS),
+        jnp.concatenate([wz, wz], axis=0),
+        jnp.concatenate([sy, sy], axis=1),
+        jnp.concatenate([sz, sz], axis=0),
+    )
 
 
 def local(fixed_image, moving_image, source_list, stretch_offsets):
@@ -297,23 +437,12 @@
     second = dot_split("pxyz,wz->pxyw", first, stretch_z.astype(jnp.bfloat16))
     stretched = second.astype(jnp.bfloat16)
     warped = jnp.take(stretched, own_list, axis=0).reshape(width_x, width_y, depth)
-    stacked = jnp.stack([fixed_image, warped])
-    grown = padded_2(stacked, (("bx", 1), ("by", 2)), 1)
-    grad_moving = central(grown[1].astype(jnp.float32))
-    grad_mean = 0.5 * (central(grown[0].astype(jnp.float32)) + grad_moving)
-    fixed_f = fixed_image.astype(jnp.float32)
-    warped_f = warped.astype(jnp.float32)
-    field_u = demons(warped_f - fixed_f, grad_moving, grad_mean)
-    pieces_u = field_u.reshape(3, peers, rows_slab, width_y, depth)
-    turned = dot_split("ckxyz,yv->ckxvz", pieces_u, stretch_y.astype(jnp.bfloat16))
-    turned = dot_split("ckxvz,zw->ckxvw", turned, stretch_z.astype(jnp.bfloat16)).astype(jnp.bfloat16)
     inverse = jnp.sum(
         (own_list[None, :] == slab_ids[:, None]).astype(jnp.int32) * slab_ids[None, :], axis=1
     )
-    sending = jnp.take(turned, inverse, axis=1)
-    arriving = lax.all_to_all(sending, "by", split_axis=1, concat_axis=1, tiled=True)
+    field_u, arriving = demons(inverse.astype(jnp.int32), fixed_image, warped, stretch_y, stretch_z)
     table = asked.astype(jnp.bfloat16)
-    back = jnp.einsum("tk,ctxyz->ckxyz", table, arriving, preferred_element_type=jnp.float32)
+    back = jnp.einsum("tk,tcxyz->ckxyz", table, arriving, preferred_element_type=jnp.float32)
     back_force = back.reshape(3, width_x, width_y, depth)
     return (field_u, back_force)
 

time: 210 us -> 170 us (0.81)
  Pallas kernels: 86.3 us -> 134 us
  blocking collectives: 41.2 us -> 0 us
  other arithmetic: 22.5 us -> 6.1 us
  starting transfers between devices: 18.6 us -> 5.22 us
  waiting for transfers between devices: 14.5 us -> 7.19 us
  matrix products: 10.7 us -> 5.53 us
  local copies, waits for them, and re-layouts: 12.4 us -> 8.89 us
    pallas_call x1, Pallas kernels: 86.3 us -> 134 us  [demons(): pl.pallas_call(functools.partial(demons_kernel, grid_x, grid_y), out_shap...]
    all_to_all x1 -> x0, blocking collectives: 41.2 us -> none  [local(): lax.all_to_all(sending, 'by', split_axis=1, concat_axis=1, tiled=True)]
    ppermute x4 -> x0, starting transfers between devices: 13.3 us -> none  [the longest x2 10.1 us: padded_2(): before = lax.ppermute(last, axis, up)]
    dot_general x6 -> x2, matrix products: 8.17 us -> 1.06 us  [dot(): return jnp.einsum(spec, a, b, preferred_element_type=jnp.float32)]
    mul x1 -> x0, other arithmetic: 6.8 us -> none  [local(): grad_mean = 0.5 * (central(grown[0].astype(jnp.float32)) + grad_moving)]
    another operation x1 -> x0, other arithmetic: 5.64 us -> none  [central(): return jnp.stack([grad_x, grad_y, grad_z])]
    ppermute x4 -> x0, waiting for transfers between devices: 5.21 us -> none  [the longest x2 5.21 us: padded_2(): after = lax.ppermute(initial, axis, down)]
    gather x1 -> x0, local copies, waits for them, and re-layouts: 2.61 us -> none  [local(): sending = jnp.take(turned, inverse, axis=1)]
  transfers between devices with their start and end apart: 5 -> 1, of which waited for: 3 -> 1; matrix products, arithmetic and copies ran while one was open for 2% -> 2% of each run, Pallas kernels for 0% -> 0%
where the time goes in v1:
time: 170 us; the launch traced here: 169 us
  Pallas kernels  134 us (79%)
  local copies, waits for them, and re-layouts  8.89 us (5%)
  waiting for transfers between devices  7.19 us (4%)
  other arithmetic  6.1 us (4%)
  matrix products  5.53 us (3%)
  starting transfers between devices  5.22 us (3%)
  between operations  1.98 us (1%)
    pallas_call x1, Pallas kernels, demons(): pl.pallas_call(functools.partial(demons_kernel, grid_x, grid_y), out_shap...  134 us
    all_to_all x1, waiting for transfers between devices, local(): lax.all_to_all(outgoing, 'by', split_axis=0, concat_axis=0, tiled=True)  7.19 us
    all_to_all x1, starting transfers between devices, local(): lax.all_to_all(outgoing, 'by', split_axis=0, concat_axis=0, tiled=True)  5.22 us
    dot_general x1, matrix products, local(): jnp.einsum('tk,tcxyz->ckxyz', table, arriving, preferred_element_type=jnp...  3.99 us
    transpose x1, local copies, waits for them, and re-layouts, local(): jnp.einsum('tk,tcxyz->ckxyz', table, arriving, preferred_element_type=jnp...  3.78 us
  transfers between devices with their start and end apart: 1, of which 1 were waited for; matrix products, arithmetic and copies ran while one was open for 2% of the time, Pallas kernels for 0%

profile of v1, /device:TPU:1, one launch (start us, length us, event | category | flops | bytes accessed | tf_op | source)
XLA Modules:
  0.0 168.9 jit_solution(12503983732267818224)
XLA Ops:
  0.6 0.0 copy-start
  0.6 0.9 select_reduce_fusion
  1.6 0.3 copy-done
  1.9 0.7 gather_fusion
  2.6 0.0 copy-start.1
  2.6 1.1 broadcast_select_fusion.1
  3.8 5.2 %all-to-all-start = ((bf16[8,8,64,128]{3,2,1,0:T(8,128)(2,1)}), bf16[8,8,64,128]{3,2,1,0:T(8,128)(2,1)S(1)}, u32[]{:S(2)}, u32[]{:S(2)}) async-start(bf16[8,8,64,128]{3,2,1,0:T(8,128)(2,1)} %broadcast_select_fusion.1), calls=%async_computation | async-start | bytes 2097152 | tf_op jit(solution)/shard_map/all_to_all | solution.py:427
  9.0 0.7 compare_and_fusion
  9.7 0.6 fusion.25
  11.6 0.7 select_reduce_fusion.1.order
  12.3 0.1 maximum_convert_fusion.1
  12.4 0.7 pad_maximum_fusion.1.sy_ref
  13.0 0.1 maximum_convert_fusion
  13.1 0.6 pad_maximum_fusion.sz_ref
  13.8 7.2 %all-to-all-done = bf16[8,8,64,128]{3,2,1,0:T(8,128)(2,1)S(1)} async-done(((bf16[8,8,64,128]{3,2,1,0:T(8,128)(2,1)}), bf16[8,8,64,128]{3,2,1,0:T(8,128)(2,1)S(1)}, u32[]{:S(2)}, u32[]{:S(2)}) %all-to-all-start) | async-done | bytes 1048608 | tf_op jit(solution)/shard_map/all_to_all | solution.py:427
  21.0 0.5 fusion.11
  21.4 0.5 fusion.7
  22.0 0.5 add_convert_fusion
  22.5 0.7 gather_fusion.1
  23.3 1.1 broadcast_select_fusion
  24.4 134.0 %shard_map.77 = (f32[3,64,64,128]{3,2,1,0:T(8,128)}, bf16[8,3,8,64,128]{4,3,2,1,0:T(8,128)(2,1)}) custom-call(s32[8]{0:T(128)} %select_reduce_fusion.1.order, bf16[64,64,128]{2,1,0:T(8,128)(2,1)} %fixed_ref.1, bf16[64,64,128]{2,1,0:T(8,128)(2,1)} %bitcast.41, bf16[64,80]{1,0:T(8,128)(2,1)} %constant.59.clone.wy_ref, bf16[256,128]{1,0:T(8,128)(2,1)} %constant.62.wz_ref, ...), custom_call_target="tpu_custom_call" | custom-call | tf_op jit(solution)/shard_map/pallas_call | solution.py:370
  158.4 4.0 %fusion.2 = f32[3,8,8,64,128]{4,1,3,2,0:T(8,128)S(1)} fusion(bf16[8,3,8,64,128]{4,3,2,1,0:T(8,128)(2,1)} %get-tuple-element.6, pred[1,8,8]{2,1,0:T(8,128)(4,1)S(1)} %get-tuple-element.10), kind=kOutput, calls=%fused_computation.6 | convolution fusion | flops 25165952 | bytes 9437248 | tf_op jit(solution)/shard_map/tk,tcxyz->ckxyz/dot_general | solution.py:445
  162.4 3.8 %copy.12 = f32[3,8,8,64,128]{4,3,2,1,0:T(8,128)} copy(f32[3,8,8,64,128]{4,1,3,2,0:T(8,128)S(1)} %fusion.2) | data formatting | bytes 12582912 | tf_op jit(solution)/shard_map/tk,tcxyz->ckxyz/transpose | solution.py:445
  166.2 2.7 %copy.22 = f32[3,64,64,128]{3,2,1,0:T(8,128)} copy(f32[3,64,64,128]{3,2,1,0:T(8,128)S(1)} %bitcast.39) | data formatting | bytes 12582912
  (15 shorter events, 0.1 us)
Async XLA Ops:
  0.6 1.2 copy-start
  2.6 7.1 %copy-start.1 = (s32[1,1,2]{2,1,0:T(1,128)S(1)}, s32[1,1,2]{2,1,0:T(1,128)}, u32[]{:S(2)}) copy-start(s32[1,1,2]{2,1,0:T(1,128)} %param.11) | copy-start | bytes 28
  3.8 17.2 %all-to-all-start = ((bf16[8,8,64,128]{3,2,1,0:T(8,128)(2,1)}), bf16[8,8,64,128]{3,2,1,0:T(8,128)(2,1)S(1)}, u32[]{:S(2)}, u32[]{:S(2)}) async-start(bf16[8,8,64,128]{3,2,1,0:T(8,128)(2,1)} %broadcast_select_fusion.1), calls=%async_computation | async-start | bytes 2097152 | tf_op jit(solution)/shard_map/all_to_all | solution.py:427
  158.4 7.8 %slice-start = ((s8[6291456]{0:T(1024)(128)(4,1)}), s8[4194304]{0:T(1024)(128)(4,1)S(1)}, s32[]{:S(2)}) async-start(s8[6291456]{0:T(1024)(128)(4,1)} %bitcast.38), calls=%async_computation.1 | async-start | bytes 8388608
  162.4 3.8 %slice-start.1 = ((s8[6291456]{0:T(1024)(128)(4,1)}), s8[2097152]{0:T(1024)(128)(4,1)S(1)}, s32[]{:S(2)}) async-start(s8[6291456]{0:T(1024)(128)(4,1)} %bitcast.38), calls=%async_computation.2 | async-start | bytes 4194304

commit v2 on v1

--- a/solution.py
+++ b/solution.py
@@ -63,6 +63,18 @@
     return dot(spec, high, w) + dot(spec, low, w)
 
 
+def unrolled(start, stop, most=4):
+    size = max(u for u in (1, 2, 4) if u <= most and (stop - start) % u == 0)
+
+    def wrap(body):
+        @pl.loop(0, (stop - start) // size)
+        def _(t):
+            for r in range(size):
+                body(start + t * size + r)
+
+    return wrap
+
+
 def demons_kernel(nx, ny, order, fixed_ref, warped_ref, wy_ref, wz_ref, sy_ref, sz_ref, u_ref, back_ref, d0_ref, gm_ref, gn_ref, tsend, esx, erx, esy, ery, ess, ers, tss, trs, own_sem, zs, xs, xsend, xrecv, ysend, yrecv, xss, xrs, yss, yrs):
     comps, width_x, width_y, depth = gm_ref.shape
     ix, iy = lax.axis_index("bx"), lax.axis_index("by")
@@ -141,7 +153,7 @@
     at_y = lax.broadcasted_iota(jnp.int32, (width_y, depth), 0)
     at_z = lax.broadcasted_iota(jnp.int32, (width_y, depth), 1)
 
-    @pl.loop(0, width_x)
+    @unrolled(0, width_x, 2)
     def _(x):
         both = []
         for m in range(2):
@@ -224,7 +236,7 @@
     blocks_x, blocks_y = width_x // R, width_y // R
     for it in range(ITERS):
 
-        @pl.loop(0, 2 * half)
+        @unrolled(0, 2 * half)
         def _(p):
             force_pair(2 * (p + (p // half) * (pairs - 2 * half)), it)
 
@@ -234,7 +246,7 @@
                 xsend[it, side, c] = zs[c, at : at + R].astype(jnp.bfloat16)
                 start("bx", it, side, c)
 
-        @pl.loop(half, pairs - half)
+        @unrolled(half, pairs - half)
         def _(p):
             force_pair(2 * p, it)
 
@@ -247,7 +259,7 @@
                     copy("bx", it, 1 - side, c).wait_recv()
                     zs[c, at : at + R] = xrecv[it, side, c].astype(jnp.float32)
 
-            @pl.loop(0, blocks_x * blocks_y)
+            @unrolled(0, blocks_x * blocks_y)
             def _(t):
                 x0 = (t // blocks_y) * R
                 y0 = pl.multiple_of((t % blocks_y) * R, R)
@@ -280,7 +292,7 @@
                         got = yrecv[it, side, c, pl.ds(t * half, half)].astype(jnp.float32)
                         xs[c, pl.ds(t * R, R), at : at + R, :] = got.reshape(R, R, depth)
 
-    @pl.loop(0, pairs)
+    @unrolled(0, pairs)
     def _(p):
         field = field_pair(2 * p)
         for r in range(2):
@@ -296,7 +308,7 @@
     def turn(d):
         first_row = order[d] * slab
 
-        @pl.loop(0, slab // 2)
+        @unrolled(0, slab // 2)
         def _(p):
             x = first_row + 2 * p
             rows = jnp.concatenate([u_ref[c, x + r] for c in range(comps) for r in range(2)], axis=1)
@@ -412,6 +424,29 @@
     )
 
 
+def sum_kernel(wanted, slabs_ref, out_ref):
+    out_ref[...] = jnp.zeros(out_ref.shape, jnp.float32)
+    for t in range(slabs_ref.shape[0]):
+
+        @pl.when(wanted[t] == pl.program_id(0))
+        def _():
+            out_ref[...] += slabs_ref[t].astype(jnp.float32)
+
+
+def slab_sums(wanted, slabs):
+    peers, comps, rows, width_y, depth = slabs.shape
+    return pl.pallas_call(
+        sum_kernel,
+        out_shape=jax.ShapeDtypeStruct((comps, peers * rows, width_y, depth), jnp.float32),
+        grid_spec=pltpu.PrefetchScalarGridSpec(
+            num_scalar_prefetch=1,
+            grid=(peers,),
+            in_specs=[pl.BlockSpec(slabs.shape, lambda k, ids: (0, 0, 0, 0, 0), pipeline_mode=pl.Buffered(1))],
+            out_specs=pl.BlockSpec((comps, rows, width_y, depth), lambda k, ids: (0, k, 0, 0)),
+        ),
+    )(wanted, slabs)
+
+
 def local(fixed_image, moving_image, source_list, stretch_offsets):
     width_x, width_y, depth = fixed_image.shape
     peers = lax.axis_size("by")
@@ -441,9 +476,7 @@
         (own_list[None, :] == slab_ids[:, None]).astype(jnp.int32) * slab_ids[None, :], axis=1
     )
     field_u, arriving = demons(inverse.astype(jnp.int32), fixed_image, warped, stretch_y, stretch_z)
-    table = asked.astype(jnp.bfloat16)
-    back = jnp.einsum("tk,tcxyz->ckxyz", table, arriving, preferred_element_type=jnp.float32)
-    back_force = back.reshape(3, width_x, width_y, depth)
+    back_force = slab_sums(wanted.astype(jnp.int32), arriving)
     return (field_u, back_force)
 
 

time: 170 us -> 148 us (0.87)
  Pallas kernels: 134 us -> 116 us
  matrix products: 5.53 us -> 1.54 us
    pallas_call x1, Pallas kernels: 134 us -> 109 us  [demons(): pl.pallas_call(functools.partial(demons_kernel, grid_x, grid_y), out_shap...]
    pallas_call x0 -> x1, Pallas kernels: none -> 7.08 us  [slab_sums(): pl.pallas_call(sum_kernel, out_shape=jax.ShapeDtypeStruct((comps, peers *...]
    dot_general x1 -> x0, matrix products: 3.99 us -> none  [local(): jnp.einsum('tk,tcxyz->ckxyz', table, arriving, preferred_element_type=jnp...]
    unnamed x9 -> x7, local copies, waits for them, and re-layouts: 3.03 us -> 6.93 us
    transpose x1 -> x0, local copies, waits for them, and re-layouts: 3.78 us -> none  [local(): jnp.einsum('tk,tcxyz->ckxyz', table, arriving, preferred_element_type=jnp...]
where the time goes in v2:
time: 148 us; the launch traced here: 147 us
  Pallas kernels  116 us (78%)
  local copies, waits for them, and re-layouts  9.01 us (6%)
  waiting for transfers between devices  7.21 us (5%)
  other arithmetic  6.04 us (4%)
  starting transfers between devices  5.22 us (4%)
  between operations  2.01 us (1%)
  matrix products  1.54 us (1%)
    pallas_call x1, Pallas kernels, demons(): pl.pallas_call(functools.partial(demons_kernel, grid_x, grid_y), out_shap...  109 us
    all_to_all x1, waiting for transfers between devices, local(): lax.all_to_all(outgoing, 'by', split_axis=0, concat_axis=0, tiled=True)  7.21 us
    pallas_call x1, Pallas kernels, slab_sums(): pl.pallas_call(sum_kernel, out_shape=jax.ShapeDtypeStruct((comps, peers *...  7.08 us
    unnamed x7, local copies, waits for them, and re-layouts  6.93 us
    all_to_all x1, starting transfers between devices, local(): lax.all_to_all(outgoing, 'by', split_axis=0, concat_axis=0, tiled=True)  5.22 us
  transfers between devices with their start and end apart: 1, of which 1 were waited for; matrix products, arithmetic and copies ran while one was open for 2% of the time, Pallas kernels for 0%

profile of v2, /device:TPU:1, one launch (start us, length us, event | category | flops | bytes accessed | tf_op | source)
XLA Modules:
  0.0 147.5 jit_solution(3161682010917457590)
XLA Ops:
  0.6 0.0 copy-start
  0.6 0.9 select_reduce_fusion.wanted
  1.6 0.3 copy-done
  1.9 0.7 gather_fusion
  2.6 0.0 copy-start.2
  2.6 1.1 broadcast_select_fusion.1
  3.8 0.0 copy-done.1
  3.8 5.2 %all-to-all-start = ((bf16[8,8,64,128]{3,2,1,0:T(8,128)(2,1)}), bf16[8,8,64,128]{3,2,1,0:T(8,128)(2,1)S(1)}, u32[]{:S(2)}, u32[]{:S(2)}) async-start(bf16[8,8,64,128]{3,2,1,0:T(8,128)(2,1)} %broadcast_select_fusion.1), calls=%async_computation | async-start | bytes 2097152 | tf_op jit(solution)/shard_map/all_to_all | solution.py:462
  9.0 0.7 compare_and_fusion
  9.7 0.6 fusion.18
  11.6 0.6 select_reduce_fusion.1.order
  12.3 0.1 maximum_convert_fusion.1
  12.3 0.7 pad_maximum_fusion.1.sy_ref
  13.0 0.1 maximum_convert_fusion
  13.1 0.6 pad_maximum_fusion.sz_ref
  13.8 7.2 %all-to-all-done = bf16[8,8,64,128]{3,2,1,0:T(8,128)(2,1)S(1)} async-done(((bf16[8,8,64,128]{3,2,1,0:T(8,128)(2,1)}), bf16[8,8,64,128]{3,2,1,0:T(8,128)(2,1)S(1)}, u32[]{:S(2)}, u32[]{:S(2)}) %all-to-all-start) | async-done | bytes 1048608 | tf_op jit(solution)/shard_map/all_to_all | solution.py:462
  21.0 0.5 fusion.6
  21.4 0.5 fusion.2
  22.0 0.5 add_convert_fusion
  22.5 0.7 gather_fusion.1
  23.3 1.1 broadcast_select_fusion
  24.4 109.4 %shard_map.77 = (f32[3,64,64,128]{3,2,1,0:T(8,128)}, bf16[8,3,8,64,128]{4,3,2,1,0:T(8,128)(2,1)}) custom-call(s32[8]{0:T(128)} %select_reduce_fusion.1.order, bf16[64,64,128]{2,1,0:T(8,128)(2,1)} %fixed_ref.1, bf16[64,64,128]{2,1,0:T(8,128)(2,1)} %bitcast.28, bf16[64,80]{1,0:T(8,128)(2,1)} %constant.59.clone.wy_ref, bf16[256,128]{1,0:T(8,128)(2,1)} %constant.62.wz_ref, ...), custom_call_target="tpu_custom_call" | custom-call | tf_op jit(solution)/shard_map/pallas_call | solution.py:382
  133.8 7.1 %shard_map.78 = f32[3,64,64,128]{3,2,1,0:T(8,128)} custom-call(s32[8]{0:T(128)} %copy-done.1, bf16[8,3,8,64,128]{4,3,2,1,0:T(8,128)(2,1)} %get-tuple-element.6.slabs_ref), custom_call_target="tpu_custom_call" | custom-call | tf_op jit(solution)/shard_map/pallas_call | solution.py:438
  140.8 6.6 %copy.11 = f32[3,64,64,128]{3,2,1,0:T(8,128)} copy(f32[3,64,64,128]{3,2,1,0:T(8,128)} %get-tuple-element.13) | data formatting | bytes 12582912
  (11 shorter events, 0.1 us)
Async XLA Ops:
  0.6 1.2 copy-start
  1.5 2.2 %copy-start.1 = (s32[8]{0:T(128)}, s32[8]{0:T(128)S(1)}, u32[]{:S(2)}) copy-start(s32[8]{0:T(128)S(1)} %select_reduce_fusion.wanted) | copy-start | bytes 100
  2.6 7.1 %copy-start.2 = (s32[1,1,2]{2,1,0:T(1,128)S(1)}, s32[1,1,2]{2,1,0:T(1,128)}, u32[]{:S(2)}) copy-start(s32[1,1,2]{2,1,0:T(1,128)} %param.11) | copy-start | bytes 28
  3.8 17.2 %all-to-all-start = ((bf16[8,8,64,128]{3,2,1,0:T(8,128)(2,1)}), bf16[8,8,64,128]{3,2,1,0:T(8,128)(2,1)S(1)}, u32[]{:S(2)}, u32[]{:S(2)}) async-start(bf16[8,8,64,128]{3,2,1,0:T(8,128)(2,1)} %broadcast_select_fusion.1), calls=%async_computation | async-start | bytes 2097152 | tf_op jit(solution)/shard_map/all_to_all | solution.py:462
